TPU v7x, 32 devices: a whole 2x2x4 slice. The times are simulated.
32 devices in a mesh: rep: 2 (over y), step: 4 (over z), patch: 4 (over x, core).
Axes of the slice: x: 2, y: 2, z: 4, core: 2. Of those that a mesh axis runs over, the one named last changes fastest.
Arguments:
- latent_old: float32 [8, 1024, 64], P(('rep', 'step'), 'patch'), parts along dimension 0, may hold values from -6 to 6
- noise_start: float32 [2048, 64], P(('rep', 'patch')), parts along dimension 0, may hold values from -6 to 6
- step_index: int32 [8], P(('rep', 'step')), parts along dimension 0, may hold values from 0 to 998
- sigma_table: float32 [1000], replicated, may hold values from 0.02 to 1
- mod_weight: bfloat16 [256, 9216], replicated, may hold values from -0.375 to 0.375
- embed_weight: bfloat16 [64, 3072], replicated, may hold values from -0.75 to 0.75
- embed_bias: float32 [3072], replicated, may hold values from -3 to 3
- query_weight: bfloat16 [3072, 1536], P('step'), may hold values from -0.109375 to 0.109375
- query_gain: float32 [128], replicated, may hold values from 0.1 to 1.9
- stale_keys: bfloat16 [8, 1280, 1536], P(('rep', 'step'), 'patch'), parts along dimension 0, may hold values from -640 to 640
- stale_values: bfloat16 [8, 1280, 1536], P(('rep', 'step'), 'patch'), parts along dimension 0, may hold values from -6 to 6
- out_weight: bfloat16 [3072, 1536], P('step'), may hold values from -0.3125 to 0.3125
- final_weight: bfloat16 [3072, 64], replicated, may hold values from -0.109375 to 0.109375
Outputs:
- latent_new: float32 [8, 1024, 64], P(('rep', 'step'), 'patch'), parts along dimension 0
There are 2 independent parts, one for each index of `rep`. A program takes and returns all parts, laid end to end along the dimension named above; an argument that names none is the same for every part. Nothing has to cross between parts.
All inputs are finite; a program needn't handle non-finite values.
Results may differ from a plain program's by a relative error of at most 0.012.
The roundings to bfloat16 on the way count: a program that leaves them out, or rounds other values in their place, can miss the bound.
Values may be sent and summed in bfloat16 or wider, within the bound.
A program may use at most 128 MiB of HBM per device.

v0:
```python
import math
import jax
import jax.numpy as jnp
from jax import lax
from jax.sharding import PartitionSpec as P

D = 3072
HEAD = 128
FREQ = 256
HEADS = 12
epsilon = 1e-06


def entering(shard, axis, join, neutral):
    place = lax.axis_index(axis)
    gathered = lax.all_gather(shard.astype(jnp.bfloat16), axis)
    state = jnp.zeros_like(shard) + jnp.asarray(neutral, shard.dtype)

    def one(hop, state):
        return join(state, lax.dynamic_index_in_dim(gathered, hop, 0, False).astype(shard.dtype))

    return lax.fori_loop(0, place, one, state)


def layer_norm(values_in):
    row_mean = jnp.mean(values_in, axis=-1, keepdims=True)
    centered = values_in - row_mean
    row_var = jnp.mean(centered * centered, axis=-1, keepdims=True)
    return centered * lax.rsqrt(row_var + epsilon)


def time_embed(sigma_now):
    half_count = FREQ // 2
    frequency = jnp.exp(
        -math.log(10000.0) * jnp.arange(half_count).astype(jnp.float32) / half_count
    )
    angles = 1000.0 * sigma_now * frequency
    return jnp.concatenate([jnp.cos(angles), jnp.sin(angles)])


def project_back(attended, weight_rows):
    return lax.dot_general(
        attended, weight_rows, (((1,), (1,)), ((), ())), preferred_element_type=jnp.float32
    )


def norm_queries(raw_queries, query_gain):
    token_count = raw_queries.shape[0]
    head_count = raw_queries.shape[1] // HEAD
    queries = raw_queries.reshape(token_count, head_count, HEAD)
    queries = (
        queries
        * lax.rsqrt(jnp.mean(queries * queries, axis=-1, keepdims=True) + epsilon)
        * query_gain
    )
    return queries.astype(jnp.bfloat16)


def empty_state(queries):
    token_count = queries.shape[0]
    head_count = queries.shape[1]
    return (
        jnp.full((head_count, token_count), -jnp.inf, jnp.float32),
        jnp.zeros((head_count, token_count), jnp.float32),
        jnp.zeros((head_count, token_count, HEAD), jnp.float32),
    )


def attend_block(queries, state_tuple, key_piece, value_piece):
    head_count = queries.shape[1]
    row_count = key_piece.shape[0]
    key_split = key_piece.reshape(row_count, head_count, HEAD)
    value_split = value_piece.reshape(row_count, head_count, HEAD)
    run_peak, run_total, run_sum = state_tuple
    scores = jnp.einsum(
        "qhd,khd->hqk", queries, key_split, preferred_element_type=jnp.float32
    ) / math.sqrt(HEAD)
    new_peak = jnp.max(scores, axis=-1)
    rescale = jnp.exp(run_peak - new_peak)
    exp_weights = jnp.exp(scores - new_peak[..., None])
    run_total = run_total * rescale + jnp.sum(exp_weights, axis=-1)
    run_sum = run_sum * rescale[..., None] + jnp.einsum(
        "hqk,khd->hqd",
        exp_weights.astype(jnp.bfloat16),
        value_split,
        preferred_element_type=jnp.float32,
    )
    return (new_peak, run_total, run_sum)


def finish_heads(state_tuple):
    final_peak, final_total, final_sum = state_tuple
    blended = final_sum / final_total[..., None]
    token_count = blended.shape[1]
    return jnp.transpose(blended, (1, 0, 2)).reshape(token_count, -1).astype(jnp.bfloat16)


def per_device(
    latent_old,
    noise_start,
    step_index,
    sigma_table,
    mod_weight,
    embed_weight,
    embed_bias,
    query_weight,
    query_gain,
    stale_keys,
    stale_values,
    out_weight,
    final_weight,
):
    step_slot = step_index[0]
    table_slots = jnp.arange(sigma_table.shape[0])
    sigma_now = jnp.sum(jnp.where(table_slots == step_slot, sigma_table, 0.0))
    sigma_next = jnp.sum(jnp.where(table_slots == step_slot + 1, sigma_table, 0.0))
    embedded = jax.nn.silu(time_embed(sigma_now)).astype(jnp.bfloat16)
    modulate = jnp.dot(embedded[None, :], mod_weight, preferred_element_type=jnp.float32)[0]
    width = D
    shift_vec = modulate[:width]
    scale_vec = modulate[width : 2 * width]
    gate_vec = modulate[2 * width :]
    latent = latent_old[0]
    token_count = latent.shape[0]
    hidden = (
        jnp.dot(latent.astype(jnp.bfloat16), embed_weight, preferred_element_type=jnp.float32)
        + embed_bias
    )
    normed = (layer_norm(hidden) * (1.0 + scale_vec) + shift_vec).astype(jnp.bfloat16)
    patch_count = lax.axis_size("patch")
    group_width = HEADS // patch_count * HEAD
    patch_slot = lax.axis_index("patch")
    query_columns = lax.dynamic_slice_in_dim(query_weight, patch_slot * group_width, group_width, 1)
    normed_every = lax.all_gather(normed, "patch", axis=0, tiled=True)
    raw_every = jnp.dot(
        normed_every,
        lax.all_gather(query_columns, "step", axis=0, tiled=True),
        preferred_element_type=jnp.float32,
    )
    queries_every = norm_queries(raw_every, query_gain)
    keys_group, values_group = (
        lax.all_to_all(stale_keys[0], "patch", split_axis=1, concat_axis=0, tiled=True),
        lax.all_to_all(stale_values[0], "patch", split_axis=1, concat_axis=0, tiled=True),
    )
    state_every = attend_block(queries_every, empty_state(queries_every), keys_group, values_group)
    attended_every = finish_heads(state_every)
    attended = lax.all_to_all(attended_every, "patch", split_axis=0, concat_axis=1, tiled=True)
    branch = project_back(attended, lax.all_gather(out_weight, "step", axis=0, tiled=True))
    mixed = hidden + gate_vec * branch
    velocity = jnp.dot(
        layer_norm(mixed).astype(jnp.bfloat16), final_weight, preferred_element_type=jnp.float32
    )
    drift_term = velocity * (sigma_next - sigma_now)
    flat_term = drift_term.reshape(-1, 128)

    def add_terms(earlier, later):
        return earlier + later

    prefix = entering(flat_term, "step", add_terms, jnp.zeros_like(flat_term))
    result = noise_start + (prefix + flat_term).reshape(token_count, -1)
    return result[None]


def solution(mesh):
    placed = (
        P(("rep", "step"), "patch", None),
        P(("rep", "patch"), None),
        P(("rep", "step")),
        P(),
        P(),
        P(),
        P(),
        P("step", None),
        P(),
        P(("rep", "step"), "patch", None),
        P(("rep", "step"), "patch", None),
        P("step", None),
        P(),
    )
    return jax.shard_map(
        per_device,
        mesh=mesh,
        in_specs=placed,
        out_specs=P(("rep", "step"), "patch", None),
        check_vma=False,
    )
```

profile of v0, /device:TPU:0, one launch (start us, length us, event | category | flops | bytes accessed | tf_op | source)
XLA Modules:
  0.0 305.8 jit_solution(14107807590935253234)
XLA Ops:
  6.5 0.0 copy-start
  6.5 0.0 all-gather.6.cloned.1.call-start
  6.5 1.7 copy-done
  8.2 0.9 constant_dynamic-slice_fusion
  9.1 0.0 all-gather.6.cloned.1.call-update
  9.1 0.0 all-gather.4.cloned.1.call-start
  9.8 1.4 select_reduce_fusion
  11.9 0.0 copy-start.2
  12.0 1.8 fusion.27
  13.8 0.5 multiply_reduce_fusion.2
  14.3 0.2 copy-done.2
  14.5 0.7 fusion.30
  15.2 1.8 add_convert_fusion
  17.0 0.0 all-gather.4.cloned.1.call-update
  17.0 0.0 all-gather.8.cloned.1.call-start
  17.1 0.7 all-gather.8.cloned.1.call-update
  17.8 2.7 all_to_all.36
  20.5 2.3 copy.38
  22.8 4.2 %all-to-all-start = ((bf16[320,4,384]{2,0,1:T(8,128)(2,1)}), bf16[320,4,384]{2,0,1:T(8,128)(2,1)}, u32[]{:S(2)}, u32[]{:S(2)}) async-start(bf16[320,4,384]{2,0,1:T(8,128)(2,1)} %copy.38), calls=%async_computation | async-start | bytes 1966080 | tf_op jit(solution)/shard_map/all_to_all | solution.py:142
  27.0 2.7 all_to_all.39
  29.7 2.3 copy.41
  32.0 9.4 %all-to-all-done = bf16[320,4,384]{2,0,1:T(8,128)(2,1)} async-done(((bf16[320,4,384]{2,0,1:T(8,128)(2,1)}), bf16[320,4,384]{2,0,1:T(8,128)(2,1)}, u32[]{:S(2)}, u32[]{:S(2)}) %all-to-all-start) | async-done | bytes 983072 | tf_op jit(solution)/shard_map/all_to_all | solution.py:142
  41.5 4.4 %all-to-all-start.1 = ((bf16[320,4,384]{2,0,1:T(8,128)(2,1)}), bf16[320,4,384]{2,0,1:T(8,128)(2,1)}, u32[]{:S(2)}, u32[]{:S(2)}) async-start(bf16[320,4,384]{2,0,1:T(8,128)(2,1)} %copy.41), calls=%async_computation.1 | async-start | bytes 1966080 | tf_op jit(solution)/shard_map/all_to_all | solution.py:143
  45.9 3.7 %reshape.109 = bf16[1280,3,128]{2,1,0:T(4,128)(2,1)} reshape(bf16[4,320,384]{2,1,0:T(8,128)(2,1)} %bitcast.5) | data formatting | bytes 1966080 | tf_op jit(solution)/shard_map/reshape | solution.py:72
  49.6 9.9 %all-to-all-done.1 = bf16[320,4,384]{2,0,1:T(8,128)(2,1)} async-done(((bf16[320,4,384]{2,0,1:T(8,128)(2,1)}), bf16[320,4,384]{2,0,1:T(8,128)(2,1)}, u32[]{:S(2)}, u32[]{:S(2)}) %all-to-all-start.1) | async-done | bytes 983072 | tf_op jit(solution)/shard_map/all_to_all | solution.py:143
  59.5 3.7 %reshape.110 = bf16[1280,3,128]{2,1,0:T(4,128)(2,1)} reshape(bf16[4,320,384]{2,1,0:T(8,128)(2,1)} %bitcast.7) | data formatting | bytes 1966080 | tf_op jit(solution)/shard_map/reshape | solution.py:73
  63.2 0.0 all-gather.6.cloned.1.call-done
  63.2 45.6 %all-gather.4.cloned.1.call-done = bf16[1024,3072]{1,0:T(8,128)(2,1)} async-done(((bf16[256,3072]{1,0:T(8,128)(2,1)}), bf16[1024,3072]{1,0:T(8,128)(2,1)}) %all-gather.4.cloned.1.call-update) | async-done | bytes 6291472 | tf_op jit(solution)/shard_map/all_gather | solution.py:134
  108.7 7.3 %fusion.31 = f32[1024,384]{0,1:T(8,128)} fusion(bf16[1024,3072]{1,0:T(8,128)(2,1)} %all-gather.4.cloned.1.call-done, bf16[3072,384]{1,0:T(8,128)(2,1)} %all-gather.6.cloned.1.call-done), kind=kOutput, calls=%fused_computation.57 | convolution fusion | flops 2415919104 | bytes 10223616 | tf_op jit(solution)/shard_map/dot_general | solution.py:135
  116.0 0.0 copy-start.6
  116.0 3.3 %copy.37 = f32[1024,3,128]{2,0,1:T(8,128)} copy(f32[1024,3,128]{0,2,1:T(8,128)} %bitcast.44) | data formatting | bytes 3145728 | tf_op jit(solution)/shard_map/reshape | solution.py:50
  119.3 1.8 multiply_reduce_fusion.3
  121.1 0.0 copy-done.6
  121.1 4.4 %multiply_reduce_fusion = (f32[3,1024]{1,0:T(4,128)S(1)}, f32[3,1024,1280]{2,1,0:T(8,128)S(1)}) fusion(bf16[1280,3,128]{2,1,0:T(4,128)(2,1)} %reshape.109, f32[1024,3,128]{2,0,1:T(8,128)} %copy.37, f32[128]{0:T(128)S(1)} %copy-done.6, f32[1024,3]{0,1:T(4,128)S(1)} %add_rsqrt_fusion), kind=kOutput, calls=%fused_computation.2 | convolution fusion | flops 1015673856 | bytes 18309632 | tf_op jit(solution)/shard_map/qhd,khd->hqk/dot_general | solution.py:75
  125.5 0.0 copy-start.3
  125.6 3.3 %fusion = f32[3,1024]{1,0:T(4,128)S(1)} fusion(f32[3,1024,1280]{2,1,0:T(8,128)S(1)} %get-tuple-element.45, f32[3,1024]{1,0:T(4,128)S(1)} %get-tuple-element.44), kind=kLoop, calls=%fused_computation.3 | loop fusion | flops 11793408 | bytes 15753216 | tf_op jit(solution)/shard_map/reduce_sum | solution.py:81
  128.9 0.0 copy-done.3
  128.9 4.5 %fusion.9 = bf16[1024,3,128]{2,0,1:T(8,128)(2,1)} fusion(f32[3,1024,1280]{2,1,0:T(8,128)S(1)} %get-tuple-element.45, f32[3,1024]{1,0:T(4,128)S(1)} %get-tuple-element.44, bf16[1280,3,128]{2,1,0:T(4,128)(2,1)S(1)} %copy-done.3, f32[1024,3]{0,1:T(4,128)S(1)} %bitcast_add_fusion.1, f32[1024,3]{0,1:T(4,128)S(1)} %multiply_bitcast_fusion), kind=kOutput, calls=%fused_computation.18 | convolution fusion | flops 1019609088 | bytes 17534976 | tf_op jit(solution)/shard_map/hqk,khd->hqd/dot_general | solution.py:82
  133.4 0.0 copy-start.5
  133.4 2.3 copy.44
  135.7 2.6 convert_element_type.59
  138.3 2.1 copy.45
  140.5 4.2 %all-to-all-start.2 = ((bf16[4,256,384]{1,2,0:T(8,128)(2,1)}), bf16[4,256,384]{1,2,0:T(8,128)(2,1)}, u32[]{:S(2)}, u32[]{:S(2)}) async-start(bf16[4,256,384]{1,2,0:T(8,128)(2,1)} %copy.45), calls=%async_computation.2 | async-start | bytes 1572864 | tf_op jit(solution)/shard_map/all_to_all | solution.py:147
  145.9 0.0 copy-done.5
  146.0 0.1 copy.48
  146.1 10.3 %all-to-all-done.2 = bf16[4,256,384]{1,2,0:T(8,128)(2,1)} async-done(((bf16[4,256,384]{1,2,0:T(8,128)(2,1)}), bf16[4,256,384]{1,2,0:T(8,128)(2,1)}, u32[]{:S(2)}, u32[]{:S(2)}) %all-to-all-start.2) | async-done | bytes 786464 | tf_op jit(solution)/shard_map/all_to_all | solution.py:147
  156.4 120.7 %all-gather.8.cloned.1.call-done = bf16[3072,1536]{1,0:T(8,128)(2,1)} async-done(((bf16[768,1536]{1,0:T(8,128)(2,1)}), bf16[3072,1536]{1,0:T(8,128)(2,1)}) %all-gather.8.cloned.1.call-update) | async-done | bytes 9437200 | tf_op jit(solution)/shard_map/all_gather | solution.py:148
  277.1 5.6 %fusion.28 = (f32[256]{0:T(256)S(1)}, f32[256,3072]{1,0:T(8,128)S(1)}) fusion(f32[256,3072]{1,0:T(8,128)S(1)} %get-tuple-element.43, bf16[256,1536]{0,1:T(8,128)(2,1)} %bitcast.11, bf16[3072,1536]{1,0:T(8,128)(2,1)} %all-gather.8.cloned.1.call-done, f32[3072]{0:T(1024)S(1)} %get-tuple-element.39), kind=kOutput, calls=%fused_computation.54 | convolution fusion | flops 2418278144 | bytes 16528384 | tf_op jit(solution)/shard_map/dot_general | solution.py:42
  282.7 0.0 copy-start.4
  282.8 0.5 multiply_reduce_fusion.1
  283.2 0.0 copy-start.1
  283.2 0.5 copy-done.4
  283.7 0.7 fusion.29
  284.4 0.1 copy.46
  284.5 0.1 convert_element_type.62
  284.7 13.6 %all_gather.16 = bf16[4,128,128]{2,1,0:T(8,128)(2,1)S(1)} all-gather(bf16[1,128,128]{2,1,0:T(8,128)(2,1)S(1)} %convert_element_type.62), channel_id=1, replica_groups=mesh['rep'=2,'step'=4,'patch'=4] {'step'}, dimensions={0}, use_global_device_ids=true | all-gather | bytes 163840 | tf_op jit(solution)/shard_map/all_gather | solution.py:16
  298.2 0.1 copy.47
  298.3 0.1 reshape.104
  298.4 0.1 reshape.105
  298.6 0.7 copy.49
  299.3 0.0 copy-done.1
  (15 shorter events, 0.2 us)
Async XLA Ops:
  6.5 1.7 copy-start
  6.5 56.6 %all-gather.6.cloned.1.call-start = ((), (), s32[]{:S(2)}) async-start(), calls=%async_computation.4 | async-start | bytes 2949120 | tf_op jit(solution)/shard_map/all_gather | solution.py:137
  9.1 99.6 %all-gather.4.cloned.1.call-start = ((), (), s32[]{:S(2)}) async-start(), calls=%async_computation.3 | async-start | bytes 7864320 | tf_op jit(solution)/shard_map/all_gather | solution.py:134
  11.9 2.5 copy-start.2
  17.0 260.1 %all-gather.8.cloned.1.call-start = ((), (), s32[]{:S(2)}) async-start(), calls=%async_computation.5 | async-start | bytes 11796480 | tf_op jit(solution)/shard_map/all_gather | solution.py:148
  22.8 18.6 %all-to-all-start = ((bf16[320,4,384]{2,0,1:T(8,128)(2,1)}), bf16[320,4,384]{2,0,1:T(8,128)(2,1)}, u32[]{:S(2)}, u32[]{:S(2)}) async-start(bf16[320,4,384]{2,0,1:T(8,128)(2,1)} %copy.38), calls=%async_computation | async-start | bytes 1966080 | tf_op jit(solution)/shard_map/all_to_all | solution.py:142
  41.5 18.0 %all-to-all-start.1 = ((bf16[320,4,384]{2,0,1:T(8,128)(2,1)}), bf16[320,4,384]{2,0,1:T(8,128)(2,1)}, u32[]{:S(2)}, u32[]{:S(2)}) async-start(bf16[320,4,384]{2,0,1:T(8,128)(2,1)} %copy.41), calls=%async_computation.1 | async-start | bytes 1966080 | tf_op jit(solution)/shard_map/all_to_all | solution.py:143
  116.0 5.1 %copy-start.6 = (f32[128]{0:T(128)S(1)}, f32[128]{0:T(128)}, u32[]{:S(2)}) copy-start(f32[128]{0:T(128)} %param.23) | copy-start | bytes 1540
  125.5 3.4 %copy-start.3 = (bf16[1280,3,128]{2,1,0:T(4,128)(2,1)S(1)}, bf16[1280,3,128]{2,1,0:T(4,128)(2,1)}, u32[]{:S(2)}) copy-start(bf16[1280,3,128]{2,1,0:T(4,128)(2,1)} %reshape.110) | copy-start | bytes 2949124
  133.4 12.5 %copy-start.5 = (f32[256,64]{0,1:T(8,128)S(1)}, f32[256,64]{0,1:T(8,128)}, u32[]{:S(2)}) copy-start(f32[256,64]{0,1:T(8,128)} %param.16) | copy-start | bytes 196612
  140.5 15.9 %all-to-all-start.2 = ((bf16[4,256,384]{1,2,0:T(8,128)(2,1)}), bf16[4,256,384]{1,2,0:T(8,128)(2,1)}, u32[]{:S(2)}, u32[]{:S(2)}) async-start(bf16[4,256,384]{1,2,0:T(8,128)(2,1)} %copy.45), calls=%async_computation.2 | async-start | bytes 1572864 | tf_op jit(solution)/shard_map/all_to_all | solution.py:147
  282.7 1.0 copy-start.4
  283.2 16.1 %copy-start.1 = (bf16[768,1536]{1,0:T(8,128)(2,1)S(1)}, bf16[768,1536]{1,0:T(8,128)(2,1)}, u32[]{:S(2)}) copy-start(bf16[768,1536]{1,0:T(8,128)(2,1)} %param.22) | copy-start | bytes 7077892
Sparse Core Ops, SparseCore 0:
  9.2 52.7 all-gather.5
  63.6 45.1 all-gather.3
  110.3 166.7 all-gather.7
where the time goes:
time: 307 us; the launch traced here: 306 us
  waiting for transfers between devices  197 us (64%)
  local copies, waits for them, and re-layouts  32.3 us (11%)
  matrix products  25 us (8%)
  between operations  15.9 us (5%)
  blocking collectives  13.6 us (4%)
  starting transfers between devices  12.9 us (4%)
  other arithmetic  9.39 us (3%)
    all_gather x1, waiting for transfers between devices, per_device(): lax.all_gather(out_weight, 'step', axis=0, tiled=True)  121 us
    all_gather x1, waiting for transfers between devices, per_device(): normed_every = lax.all_gather(normed, 'patch', axis=0, tiled=True)  45.6 us
    all_gather x1, blocking collectives, entering(): gathered = lax.all_gather(shard.astype(jnp.bfloat16), axis)  13.6 us
    all_to_all x1, waiting for transfers between devices, per_device(): lax.all_to_all(attended_every, 'patch', split_axis=0, concat_axis=1, tile...  10.3 us
    all_to_all x1, waiting for transfers between devices, per_device(): lax.all_to_all(stale_values[0], 'patch', split_axis=1, concat_axis=0, til...  9.9 us
    all_to_all x1, waiting for transfers between devices, per_device(): lax.all_to_all(stale_keys[0], 'patch', split_axis=1, concat_axis=0, tiled...  9.43 us
    dot_general x1, matrix products, per_device(): jnp.dot(normed_every, lax.all_gather(query_columns, 'step', axis=0, tiled...  7.27 us
    convert_element_type x3, local copies, waits for them, and re-layouts, finish_heads(): jnp.transpose(blended, (1, 0, 2)).reshape(token_count, -1)  7.09 us
  transfers between devices with their start and end apart: 6, of which 5 were waited for; matrix products, arithmetic and copies ran while one was open for 16% of the time, Pallas kernels for 0%

commit v1 on v0

--- a/solution.py
+++ b/solution.py
@@ -131,7 +131,14 @@
     group_width = HEADS // patch_count * HEAD
     patch_slot = lax.axis_index("patch")
     query_columns = lax.dynamic_slice_in_dim(query_weight, patch_slot * group_width, group_width, 1)
-    normed_every = lax.all_gather(normed, "patch", axis=0, tiled=True)
+    ring = [normed]
+    for hop_ in range(3):
+        ring.append(lax.ppermute(ring[-1], "patch", [(dev, (dev + 1) % 4) for dev in range(4)]))
+    normed_every = jnp.roll(
+        jnp.concatenate(ring[::-1], axis=0),
+        (lax.axis_index("patch") + 1) * ring[0].shape[0],
+        axis=0,
+    )
     raw_every = jnp.dot(
         normed_every,
         lax.all_gather(query_columns, "step", axis=0, tiled=True),

time: 307 us -> 259 us (0.84)
  waiting for transfers between devices: 197 us -> 128 us
  local copies, waits for them, and re-layouts: 32.3 us -> 46.6 us
    all_gather x1, waiting for transfers between devices: 121 us -> 53.6 us  [per_device(): lax.all_gather(out_weight, 'step', axis=0, tiled=True)]
    all_gather x1 -> x0, waiting for transfers between devices: 45.6 us -> none  [per_device(): normed_every = lax.all_gather(normed, 'patch', axis=0, tiled=True)]
    ppermute x0 -> x3, waiting for transfers between devices: none -> 40 us  [per_device(): lax.ppermute(ring[-1], 'patch', [(dev, (dev + 1) % 4) for dev in range(4)])]
    unnamed x15 -> x33, local copies, waits for them, and re-layouts: 2.46 us -> 16.8 us
    all_to_all x1, waiting for transfers between devices: 9.43 us -> 13.7 us  [per_device(): lax.all_to_all(stale_keys[0], 'patch', split_axis=1, concat_axis=0, tiled...]
  transfers between devices with their start and end apart: 6 -> 8, of which waited for: 5 -> 6; matrix products, arithmetic and copies ran while one was open for 16% -> 26% of each run, Pallas kernels for 0% -> 0%
where the time goes in v1:
time: 259 us; the launch traced here: 258 us
  waiting for transfers between devices  128 us (49%)
  local copies, waits for them, and re-layouts  46.6 us (18%)
  matrix products  27.1 us (10%)
  between operations  16.3 us (6%)
  starting transfers between devices  15.1 us (6%)
  blocking collectives  13.6 us (5%)
  other arithmetic  11.5 us (4%)
    all_gather x1, waiting for transfers between devices, per_device(): lax.all_gather(out_weight, 'step', axis=0, tiled=True)  53.6 us
    ppermute x3, waiting for transfers between devices, per_device(): lax.ppermute(ring[-1], 'patch', [(dev, (dev + 1) % 4) for dev in range(4)])  40 us
    unnamed x33, local copies, waits for them, and re-layouts  16.8 us
    all_to_all x1, waiting for transfers between devices, per_device(): lax.all_to_all(stale_keys[0], 'patch', split_axis=1, concat_axis=0, tiled...  13.7 us
    all_gather x1, blocking collectives, entering(): gathered = lax.all_gather(shard.astype(jnp.bfloat16), axis)  13.6 us
    all_to_all x1, waiting for transfers between devices, per_device(): lax.all_to_all(attended_every, 'patch', split_axis=0, concat_axis=1, tile...  10 us
    all_to_all x1, waiting for transfers between devices, per_device(): lax.all_to_all(stale_values[0], 'patch', split_axis=1, concat_axis=0, til...  9.92 us
    dot_general x1, matrix products, per_device(): jnp.dot(normed_every, lax.all_gather(query_columns, 'step', axis=0, tiled...  7.41 us
  transfers between devices with their start and end apart: 8, of which 6 were waited for; matrix products, arithmetic and copies ran while one was open for 26% of the time, Pallas kernels for 0%

profile of v1, /device:TPU:0, one launch (start us, length us, event | category | flops | bytes accessed | tf_op | source)
XLA Modules:
  0.0 258.1 jit_solution(17617583595388173476)
XLA Ops:
  6.5 1.7 copy-done
  8.2 0.9 constant_dynamic-slice_fusion
  9.1 0.0 all-gather.3.cloned.1.call-update
  9.1 0.0 copy-start.5
  9.1 0.0 all-gather.5.cloned.1.call-start
  9.2 0.7 all-gather.5.cloned.1.call-update
  10.5 0.7 select_reduce_fusion
  11.9 3.1 %fusion.33 = f32[1,9216]{1,0:T(1,128)S(1)} fusion(bf16[256,1]{0,1:T(2,128)(2,1)S(1)} %reshape.107, bf16[256,9216]{1,0:T(8,128)(2,1)} %param.19), kind=kOutput, calls=%fused_computation.67 | convolution fusion | flops 4718592 | bytes 4755968 | tf_op jit(solution)/shard_map/dot_general | solution.py:118
  15.0 0.6 fusion.29
  15.6 1.5 fusion.30
  17.1 0.5 multiply_reduce_fusion.2
  17.6 0.0 copy-done.7
  17.6 0.7 add_convert_fusion
  18.3 0.5 collective-permute-start
  18.8 20.0 %collective-permute-done = bf16[256,3072]{1,0:T(8,128)(2,1)S(1)} collective-permute-done((bf16[256,3072]{1,0:T(8,128)(2,1)S(1)}, bf16[256,3072]{1,0:T(8,128)(2,1)S(1)}, u32[]{:S(2)}, u32[]{:S(2)}) %collective-permute-start) | collective-permute-done | bytes 1572896 | tf_op jit(solution)/shard_map/ppermute | solution.py:136
  38.8 1.1 copy-done.2
  40.0 0.0 collective-permute-start.1
  40.0 19.9 %collective-permute-done.1 = bf16[256,3072]{1,0:T(8,128)(2,1)} collective-permute-done((bf16[256,3072]{1,0:T(8,128)(2,1)S(1)}, bf16[256,3072]{1,0:T(8,128)(2,1)}, u32[]{:S(2)}, u32[]{:S(2)}) %collective-permute-start.1) | collective-permute-done | bytes 1572896 | tf_op jit(solution)/shard_map/ppermute | solution.py:136
  59.9 0.0 collective-permute-start.2
  59.9 2.7 %all_to_all.36 = bf16[320,4,384]{2,1,0:T(4,128)(2,1)} reshape(bf16[1,320,1536]{2,1,0:T(8,128)(2,1)} %param.24) | data formatting | bytes 1966080 | tf_op jit(solution)/shard_map/all_to_all | solution.py:149
  62.6 2.3 copy.38
  64.9 4.2 %all-to-all-start = ((bf16[320,4,384]{2,0,1:T(8,128)(2,1)}), bf16[320,4,384]{2,0,1:T(8,128)(2,1)}, u32[]{:S(2)}, u32[]{:S(2)}) async-start(bf16[320,4,384]{2,0,1:T(8,128)(2,1)} %copy.38), calls=%async_computation | async-start | bytes 1966080 | tf_op jit(solution)/shard_map/all_to_all | solution.py:149
  69.1 2.7 %all_to_all.39 = bf16[320,4,384]{2,1,0:T(4,128)(2,1)} reshape(bf16[1,320,1536]{2,1,0:T(8,128)(2,1)} %param.25) | data formatting | bytes 1966080 | tf_op jit(solution)/shard_map/all_to_all | solution.py:150
  71.9 2.4 copy.41
  74.3 13.7 %all-to-all-done = bf16[320,4,384]{2,0,1:T(8,128)(2,1)} async-done(((bf16[320,4,384]{2,0,1:T(8,128)(2,1)}), bf16[320,4,384]{2,0,1:T(8,128)(2,1)}, u32[]{:S(2)}, u32[]{:S(2)}) %all-to-all-start) | async-done | bytes 983072 | tf_op jit(solution)/shard_map/all_to_all | solution.py:149
  88.0 5.9 %all-to-all-start.1 = ((bf16[320,4,384]{2,0,1:T(8,128)(2,1)}), bf16[320,4,384]{2,0,1:T(8,128)(2,1)}, u32[]{:S(2)}, u32[]{:S(2)}) async-start(bf16[320,4,384]{2,0,1:T(8,128)(2,1)} %copy.41), calls=%async_computation.1 | async-start | bytes 1966080 | tf_op jit(solution)/shard_map/all_to_all | solution.py:150
  93.9 3.7 %reshape.109 = bf16[1280,3,128]{2,1,0:T(4,128)(2,1)} reshape(bf16[4,320,384]{2,1,0:T(8,128)(2,1)} %bitcast.5) | data formatting | bytes 1966080 | tf_op jit(solution)/shard_map/reshape | solution.py:72
  97.6 9.9 %all-to-all-done.1 = bf16[320,4,384]{2,0,1:T(8,128)(2,1)} async-done(((bf16[320,4,384]{2,0,1:T(8,128)(2,1)}), bf16[320,4,384]{2,0,1:T(8,128)(2,1)}, u32[]{:S(2)}, u32[]{:S(2)}) %all-to-all-start.1) | async-done | bytes 983072 | tf_op jit(solution)/shard_map/all_to_all | solution.py:150
  107.5 3.7 %reshape.110 = bf16[1280,3,128]{2,1,0:T(4,128)(2,1)} reshape(bf16[4,320,384]{2,1,0:T(8,128)(2,1)} %bitcast.7) | data formatting | bytes 1966080 | tf_op jit(solution)/shard_map/reshape | solution.py:73
  111.2 0.0 collective-permute-done.2
  111.2 2.8 %constant_dynamic-update-slice_fusion.7 = bf16[2048,3072]{1,0:T(8,128)(2,1)} fusion(bf16[256,3072]{1,0:T(8,128)(2,1)} %collective-permute-done.2), kind=kLoop, calls=%fused_computation.41 | loop fusion | bytes 3145728
  114.0 2.7 %constant_dynamic-update-slice_fusion.6 = bf16[2048,3072]{1,0:T(8,128)(2,1)} fusion(bf16[2048,3072]{1,0:T(8,128)(2,1)} %constant_dynamic-update-slice_fusion.7, bf16[256,3072]{1,0:T(8,128)(2,1)} %collective-permute-done.1), kind=kLoop, calls=%fused_computation.40 | loop fusion | bytes 3145728
  116.6 1.3 constant_dynamic-update-slice_fusion.5
  117.9 1.8 constant_dynamic-update-slice_fusion.4
  119.7 2.7 %constant_dynamic-update-slice_fusion.3 = bf16[2048,3072]{1,0:T(8,128)(2,1)} fusion(bf16[2048,3072]{1,0:T(8,128)(2,1)} %constant_dynamic-update-slice_fusion.4, bf16[256,3072]{1,0:T(8,128)(2,1)} %collective-permute-done.2), kind=kLoop, calls=%fused_computation.37 | loop fusion | bytes 3145728
  122.4 2.8 %constant_dynamic-update-slice_fusion.2 = bf16[2048,3072]{1,0:T(8,128)(2,1)} fusion(bf16[2048,3072]{1,0:T(8,128)(2,1)} %constant_dynamic-update-slice_fusion.3, bf16[256,3072]{1,0:T(8,128)(2,1)} %collective-permute-done.1), kind=kLoop, calls=%fused_computation.36 | loop fusion | bytes 3145728
  125.2 1.3 constant_dynamic-update-slice_fusion.1
  126.4 1.8 constant_dynamic-update-slice_fusion
  128.2 7.4 %fusion.6 = f32[1024,384]{0,1:T(8,128)} fusion(bf16[3072,384]{1,0:T(8,128)(2,1)} %all-gather.3.cloned.1.call-done, bf16[2048,3072]{1,0:T(8,128)(2,1)} %constant_dynamic-update-slice_fusion, s32[]{:T(128)S(6)} %select_n.29), kind=kOutput, calls=%fused_computation.8 | convolution fusion | flops 2415919104 | bytes 10223620 | tf_op jit(solution)/shard_map/dot_general | solution.py:142
  135.7 3.1 %copy.37 = f32[1024,3,128]{2,0,1:T(8,128)} copy(f32[1024,3,128]{0,2,1:T(8,128)} %bitcast.43) | data formatting | bytes 3145728 | tf_op jit(solution)/shard_map/reshape | solution.py:50
  138.8 1.6 multiply_reduce_fusion.3
  140.4 4.3 %multiply_reduce_fusion = (f32[3,1024]{1,0:T(4,128)S(1)}, f32[3,1024,1280]{2,1,0:T(8,128)S(1)}) fusion(bf16[1280,3,128]{2,1,0:T(4,128)(2,1)} %reshape.109, f32[1024,3,128]{2,0,1:T(8,128)} %copy.37, f32[128]{0:T(128)S(1)} %copy-done.12, f32[1024,3]{0,1:T(4,128)S(1)} %add_rsqrt_fusion), kind=kOutput, calls=%fused_computation.2 | convolution fusion | flops 1015673856 | bytes 18309632 | tf_op jit(solution)/shard_map/qhd,khd->hqk/dot_general | solution.py:75
  144.7 3.3 %fusion = f32[3,1024]{1,0:T(4,128)S(1)} fusion(f32[3,1024,1280]{2,1,0:T(8,128)S(1)} %get-tuple-element.45, f32[3,1024]{1,0:T(4,128)S(1)} %get-tuple-element.44), kind=kLoop, calls=%fused_computation.3 | loop fusion | flops 11793408 | bytes 15753216 | tf_op jit(solution)/shard_map/reduce_sum | solution.py:81
  148.0 4.5 %fusion.11 = bf16[1024,3,128]{2,0,1:T(8,128)(2,1)} fusion(f32[3,1024,1280]{2,1,0:T(8,128)S(1)} %get-tuple-element.45, f32[3,1024]{1,0:T(4,128)S(1)} %get-tuple-element.44, bf16[1280,3,128]{2,1,0:T(4,128)(2,1)S(1)} %copy-done.4, f32[1024,3]{0,1:T(4,128)S(1)} %bitcast_add_fusion.1, f32[1024,3]{0,1:T(4,128)S(1)} %multiply_bitcast_fusion), kind=kOutput, calls=%fused_computation.20 | convolution fusion | flops 1019609088 | bytes 17534976 | tf_op jit(solution)/shard_map/hqk,khd->hqd/dot_general | solution.py:82
  152.5 2.3 copy.44
  154.8 2.6 %convert_element_type.59 = bf16[4,256,384]{1,0,2:T(4,128)(2,1)} reshape(bf16[1024,3,128]{0,2,1:T(8,128)(2,1)} %copy.44) | data formatting | bytes 1572864 | tf_op jit(solution)/shard_map/convert_element_type | solution.py:95
  157.5 2.1 copy.45
  159.6 4.4 %all-to-all-start.2 = ((bf16[4,256,384]{1,2,0:T(8,128)(2,1)}), bf16[4,256,384]{1,2,0:T(8,128)(2,1)}, u32[]{:S(2)}, u32[]{:S(2)}) async-start(bf16[4,256,384]{1,2,0:T(8,128)(2,1)} %copy.45), calls=%async_computation.2 | async-start | bytes 1572864 | tf_op jit(solution)/shard_map/all_to_all | solution.py:154
  165.3 0.1 copy.48
  165.4 10.0 %all-to-all-done.2 = bf16[4,256,384]{1,2,0:T(8,128)(2,1)} async-done(((bf16[4,256,384]{1,2,0:T(8,128)(2,1)}), bf16[4,256,384]{1,2,0:T(8,128)(2,1)}, u32[]{:S(2)}, u32[]{:S(2)}) %all-to-all-start.2) | async-done | bytes 786464 | tf_op jit(solution)/shard_map/all_to_all | solution.py:154
  175.5 53.6 %all-gather.5.cloned.1.call-done = bf16[3072,1536]{1,0:T(8,128)(2,1)} async-done(((bf16[768,1536]{1,0:T(8,128)(2,1)}), bf16[3072,1536]{1,0:T(8,128)(2,1)}) %all-gather.5.cloned.1.call-update) | async-done | bytes 9437200 | tf_op jit(solution)/shard_map/all_gather | solution.py:155
  229.1 5.6 %fusion.31 = (f32[256]{0:T(256)S(1)}, f32[256,3072]{1,0:T(8,128)S(1)}) fusion(f32[256,3072]{1,0:T(8,128)S(1)} %get-tuple-element.43, bf16[256,1536]{0,1:T(8,128)(2,1)} %bitcast.11, bf16[3072,1536]{1,0:T(8,128)(2,1)} %all-gather.5.cloned.1.call-done, f32[3072]{0:T(1024)S(1)} %copy-done.10), kind=kOutput, calls=%fused_computation.65 | convolution fusion | flops 2418278144 | bytes 16528384 | tf_op jit(solution)/shard_map/dot_general | solution.py:42
  234.7 0.0 copy-start.6
  234.7 0.5 multiply_reduce_fusion.1
  235.2 0.0 copy-start.1
  235.2 0.5 copy-done.6
  235.7 0.7 fusion.32
  236.4 0.1 copy.46
  236.5 0.1 convert_element_type.62
  236.6 13.6 %all_gather.12 = bf16[4,128,128]{2,1,0:T(8,128)(2,1)S(1)} all-gather(bf16[1,128,128]{2,1,0:T(8,128)(2,1)S(1)} %convert_element_type.62), channel_id=1, replica_groups=mesh['rep'=2,'step'=4,'patch'=4] {'step'}, dimensions={0}, use_global_device_ids=true | all-gather | bytes 163840 | tf_op jit(solution)/shard_map/all_gather | solution.py:16
  250.2 0.1 copy.47
  250.3 0.1 reshape.104
  250.4 0.1 reshape.105
  250.5 0.7 copy.49
  (35 shorter events, 0.2 us)
Async XLA Ops:
  6.5 1.7 copy-start
  6.5 4.0 %copy-start.11 = (f32[1000]{0:T(1024)S(1)}, f32[1000]{0:T(1024)}, u32[]{:S(2)}) copy-start(f32[1000]{0:T(1024)} %param.18) | copy-start | bytes 12004
  6.5 121.7 %all-gather.3.cloned.1.call-start = ((), (), s32[]{:S(2)}) async-start(), calls=%async_computation.3 | async-start | bytes 2949120 | tf_op jit(solution)/shard_map/all_gather | solution.py:144
  9.1 6.5 %copy-start.5 = (bf16[64,3072]{1,0:T(8,128)(2,1)S(1)}, bf16[64,3072]{1,0:T(8,128)(2,1)}, u32[]{:S(2)}) copy-start(bf16[64,3072]{1,0:T(8,128)(2,1)} %param.20) | copy-start | bytes 1179652
  9.1 220.0 %all-gather.5.cloned.1.call-start = ((), (), s32[]{:S(2)}) async-start(), calls=%async_computation.4 | async-start | bytes 11796480 | tf_op jit(solution)/shard_map/all_gather | solution.py:155
  15.6 2.0 copy-start.7
  18.3 20.6 %collective-permute-start = (bf16[256,3072]{1,0:T(8,128)(2,1)S(1)}, bf16[256,3072]{1,0:T(8,128)(2,1)S(1)}, u32[]{:S(2)}, u32[]{:S(2)}) collective-permute-start(bf16[256,3072]{1,0:T(8,128)(2,1)S(1)} %add_convert_fusion), channel_id=1, source_target_pairs={{0,1},{1,2},{2,3},{3,0},{4,5},{5,6},{6,7},{7,4},{8,9},{9,10},{10,1... | collective-permute-start | bytes 4718600 | tf_op jit(solution)/shard_map/ppermute | solution.py:136
  38.8 1.1 copy-start.2
  40.0 19.9 %collective-permute-start.1 = (bf16[256,3072]{1,0:T(8,128)(2,1)S(1)}, bf16[256,3072]{1,0:T(8,128)(2,1)}, u32[]{:S(2)}, u32[]{:S(2)}) collective-permute-start(bf16[256,3072]{1,0:T(8,128)(2,1)S(1)} %collective-permute-done), channel_id=1, source_target_pairs={{0,1},{1,2},{2,3},{3,0},{4,5},{5,6},{6,7},{7,4},{8,9},{9,10},{10,1... | collective-permute-start | bytes 4718600 | tf_op jit(solution)/shard_map/ppermute | solution.py:136
  59.9 51.3 %collective-permute-start.2 = (bf16[256,3072]{1,0:T(8,128)(2,1)}, bf16[256,3072]{1,0:T(8,128)(2,1)}, u32[]{:S(2)}, u32[]{:S(2)}) collective-permute-start(bf16[256,3072]{1,0:T(8,128)(2,1)} %collective-permute-done.1), channel_id=1, source_target_pairs={{0,1},{1,2},{2,3},{3,0},{4,5},{5,6},{6,7},{7,4},{8,9},{9,10},{10,1... | collective-permute-start | bytes 4718600 | tf_op jit(solution)/shard_map/ppermute | solution.py:136
  64.9 23.1 %all-to-all-start = ((bf16[320,4,384]{2,0,1:T(8,128)(2,1)}), bf16[320,4,384]{2,0,1:T(8,128)(2,1)}, u32[]{:S(2)}, u32[]{:S(2)}) async-start(bf16[320,4,384]{2,0,1:T(8,128)(2,1)} %copy.38), calls=%async_computation | async-start | bytes 1966080 | tf_op jit(solution)/shard_map/all_to_all | solution.py:149
  88.0 19.5 %all-to-all-start.1 = ((bf16[320,4,384]{2,0,1:T(8,128)(2,1)}), bf16[320,4,384]{2,0,1:T(8,128)(2,1)}, u32[]{:S(2)}, u32[]{:S(2)}) async-start(bf16[320,4,384]{2,0,1:T(8,128)(2,1)} %copy.41), calls=%async_computation.1 | async-start | bytes 1966080 | tf_op jit(solution)/shard_map/all_to_all | solution.py:150
  111.2 5.5 %copy-start.3 = (bf16[256,3072]{1,0:T(8,128)(2,1)S(1)}, bf16[256,3072]{1,0:T(8,128)(2,1)}, u32[]{:S(2)}) copy-start(bf16[256,3072]{1,0:T(8,128)(2,1)} %copy-done.2) | copy-start | bytes 4718596
  114.0 3.9 %copy-start.8 = (f32[3072]{0:T(1024)S(1)}, f32[3072]{0:T(1024)}, u32[]{:S(2)}) copy-start(f32[3072]{0:T(1024)} %copy-done.7) | copy-start | bytes 36868
  135.7 4.7 %copy-start.12 = (f32[128]{0:T(128)S(1)}, f32[128]{0:T(128)}, u32[]{:S(2)}) copy-start(f32[128]{0:T(128)} %param.23) | copy-start | bytes 1540
  144.6 3.4 %copy-start.4 = (bf16[1280,3,128]{2,1,0:T(4,128)(2,1)S(1)}, bf16[1280,3,128]{2,1,0:T(4,128)(2,1)}, u32[]{:S(2)}) copy-start(bf16[1280,3,128]{2,1,0:T(4,128)(2,1)} %reshape.110) | copy-start | bytes 2949124
  152.5 12.8 %copy-start.9 = (f32[256,64]{0,1:T(8,128)S(1)}, f32[256,64]{0,1:T(8,128)}, u32[]{:S(2)}) copy-start(f32[256,64]{0,1:T(8,128)} %param.16) | copy-start | bytes 196612
  152.5 76.6 %copy-start.10 = (f32[3072]{0:T(1024)S(1)}, f32[3072]{0:T(1024)}, u32[]{:S(2)}) copy-start(f32[3072]{0:T(1024)} %get-tuple-element.39) | copy-start | bytes 36868
  159.6 15.9 %all-to-all-start.2 = ((bf16[4,256,384]{1,2,0:T(8,128)(2,1)}), bf16[4,256,384]{1,2,0:T(8,128)(2,1)}, u32[]{:S(2)}, u32[]{:S(2)}) async-start(bf16[4,256,384]{1,2,0:T(8,128)(2,1)} %copy.45), calls=%async_computation.2 | async-start | bytes 1572864 | tf_op jit(solution)/shard_map/all_to_all | solution.py:154
  234.7 1.0 copy-start.6
  235.2 16.1 %copy-start.1 = (bf16[768,1536]{1,0:T(8,128)(2,1)S(1)}, bf16[768,1536]{1,0:T(8,128)(2,1)}, u32[]{:S(2)}) copy-start(bf16[768,1536]{1,0:T(8,128)(2,1)} %param.22) | copy-start | bytes 7077892
Sparse Core Ops, SparseCore 0:
  9.2 52.6 all-gather.2
  63.5 165.5 all-gather.4
